TPU v7x, 256 devices: a whole 4x4x8 slice. The times are simulated.
256 devices in a mesh: task: 8 (over x, core), fsdp: 32 (over z, y).
Axes of the slice: x: 4, y: 4, z: 8, core: 2. Of those that a mesh axis runs over, the one named last changes fastest.
Arguments:
- grads_first: bfloat16 [16, 4096, 4096], P('task', 'fsdp'), may hold values from -120 to 120
- weights_first: float32 [4096, 4096], P('fsdp', 'task'), may hold values from -6 to 6
- moment_first: float32 [4096, 4096], P('fsdp', 'task'), may hold values from -3 to 3
- variance_first: float32 [4096, 4096], P('fsdp', 'task'), may hold values from 0.0025 to 1
- grads_second: bfloat16 [16, 4096, 4096], P('task', 'fsdp'), may hold values from -120 to 120
- weights_second: float32 [4096, 4096], P('fsdp', 'task'), may hold values from -6 to 6
- moment_second: float32 [4096, 4096], P('fsdp', 'task'), may hold values from -3 to 3
- variance_second: float32 [4096, 4096], P('fsdp', 'task'), may hold values from 0.0025 to 1
Outputs:
- combined_first: float32 [4096, 4096], P('fsdp', 'task')
- new_weights_first: float32 [4096, 4096], P('fsdp', 'task')
- new_moment_first: float32 [4096, 4096], P('fsdp', 'task')
- new_variance_first: float32 [4096, 4096], P('fsdp', 'task')
- combined_second: float32 [4096, 4096], P('fsdp', 'task')
- new_weights_second: float32 [4096, 4096], P('fsdp', 'task')
- new_moment_second: float32 [4096, 4096], P('fsdp', 'task')
- new_variance_second: float32 [4096, 4096], P('fsdp', 'task')
All inputs are finite; a program needn't handle non-finite values.
Results may differ from a plain program's by a relative error of at most 0.0006.
Values may be sent and summed in bfloat16 or wider, within the bound.
A program may use at most 128 MiB of HBM per device.

v0:
```python
import jax
import jax.numpy as jnp
from jax import lax
from jax.sharding import PartitionSpec as P

ITERS = 20
temper = 0.05
beta_one = 0.9
beta_two = 0.999
learn_rate = 0.001
adam_step = 1000.0
epsilon = 1e-08


def frank_wolfe(gram):
    scaled = gram / jnp.max(jnp.diagonal(gram))

    def advance(iteration, mixture):
        slope = 2.0 * jnp.dot(scaled, mixture, precision=lax.Precision.HIGHEST)
        expweights = jnp.exp(-slope / temper)
        vertex = expweights / jnp.sum(expweights)
        stepsize = 2.0 / (jnp.asarray(iteration).astype(jnp.float32) + 2.0)
        return mixture + stepsize * (vertex - mixture)

    start_mix = jnp.full((gram.shape[0],), 1.0 / gram.shape[0], jnp.float32)
    return lax.fori_loop(0, ITERS, advance, start_mix)


def adam_update(weights, moment, variance, combined):
    new_moment = beta_one * moment + (1.0 - beta_one) * combined
    new_variance = beta_two * variance + (1.0 - beta_two) * combined * combined
    corrected = new_moment / (1.0 - beta_one**adam_step)
    scaled_var = new_variance / (1.0 - beta_two**adam_step)
    new_weights = weights - learn_rate * corrected / (jnp.sqrt(scaled_var) + epsilon)
    return (new_weights, new_moment, new_variance)


def weighted_sum(mixture, stacked):
    return jnp.sum(mixture[:, None, None] * stacked.astype(jnp.float32), axis=0)


def prepare_first(gradients):
    regrouped = lax.all_to_all(gradients, "task", split_axis=2, concat_axis=0, tiled=True)
    return (
        regrouped,
        jnp.einsum("tre,sre->ts", regrouped, regrouped, preferred_element_type=jnp.float32),
    )


def prepare_second(gradients):
    regrouped = lax.all_to_all(gradients, "task", split_axis=2, concat_axis=0, tiled=True)
    return (
        regrouped,
        jnp.einsum("tre,sre->ts", regrouped, regrouped, preferred_element_type=jnp.float32),
    )


def combine_first(retained, mixture):
    return weighted_sum(mixture, retained)


def combine_second(retained, mixture):
    return weighted_sum(mixture, retained)


def local(
    grads_first,
    weights_first,
    moment_first,
    variance_first,
    grads_second,
    weights_second,
    moment_second,
    variance_second,
):
    retained_first, partial_first = prepare_first(grads_first)
    retained_second, partial_second = prepare_second(grads_second)
    gram_first, gram_second = lax.psum((partial_first, partial_second), ("task", "fsdp"))
    mixture_first = frank_wolfe(gram_first)
    mixture_second = frank_wolfe(gram_second)
    combined_first = combine_first(retained_first, mixture_first)
    first_w, first_m, first_v = adam_update(
        weights_first, moment_first, variance_first, combined_first
    )
    combined_second = combine_second(retained_second, mixture_second)
    second_w, second_m, second_v = adam_update(
        weights_second, moment_second, variance_second, combined_second
    )
    return (
        combined_first,
        first_w,
        first_m,
        first_v,
        combined_second,
        second_w,
        second_m,
        second_v,
    )


def solution(mesh):
    in_specs = (
        P("task", "fsdp", None),
        P("fsdp", "task"),
        P("fsdp", "task"),
        P("fsdp", "task"),
        P("task", "fsdp", None),
        P("fsdp", "task"),
        P("fsdp", "task"),
        P("fsdp", "task"),
    )
    out_specs = (
        P("fsdp", "task"),
        P("fsdp", "task"),
        P("fsdp", "task"),
        P("fsdp", "task"),
        P("fsdp", "task"),
        P("fsdp", "task"),
        P("fsdp", "task"),
        P("fsdp", "task"),
    )
    return jax.shard_map(local, mesh=mesh, in_specs=in_specs, out_specs=out_specs, check_vma=False)
```

profile of v0, /device:TPU:1, one launch (start us, length us, event | category | flops | bytes accessed | tf_op | source)
XLA Modules:
  0.0 235.0 jit_solution(9579224308458622726)
XLA Ops:
  0.6 6.2 %copy.25 = bf16[2,128,4096]{1,0,2:T(2,128)(2,1)} copy(bf16[2,128,4096]{2,1,0:T(8,128)(2,1)} %param.16) | data formatting | bytes 4194304 | tf_op args[4]
  6.8 6.7 %all-to-all-start.1 = ((bf16[2,128,4096]{1,0,2:T(2,128)(2,1)}), bf16[2,128,4096]{1,0,2:T(2,128)(2,1)S(1)}, u32[]{:S(2)}, u32[]{:S(2)}) async-start(bf16[2,128,4096]{1,0,2:T(2,128)(2,1)} %copy.25), calls=%async_computation.1 | async-start | bytes 4194304 | tf_op jit(solution)/shard_map/all_to_all | solution.py:51
  13.6 6.2 %copy.20 = bf16[2,128,4096]{1,0,2:T(2,128)(2,1)} copy(bf16[2,128,4096]{2,1,0:T(8,128)(2,1)} %param.12) | data formatting | bytes 4194304 | tf_op args[0]
  19.7 20.2 %all-to-all-done.1 = bf16[2,128,4096]{1,0,2:T(2,128)(2,1)S(1)} async-done(((bf16[2,128,4096]{1,0,2:T(2,128)(2,1)}), bf16[2,128,4096]{1,0,2:T(2,128)(2,1)S(1)}, u32[]{:S(2)}, u32[]{:S(2)}) %all-to-all-start.1) | async-done | bytes 2097184 | tf_op jit(solution)/shard_map/all_to_all | solution.py:51
  39.9 1.3 copy-done
  41.2 4.4 %all-to-all-start = ((bf16[2,128,4096]{1,0,2:T(2,128)(2,1)}), bf16[2,128,4096]{1,0,2:T(2,128)(2,1)S(1)}, u32[]{:S(2)}, u32[]{:S(2)}) async-start(bf16[2,128,4096]{1,0,2:T(2,128)(2,1)} %copy.20), calls=%async_computation | async-start | bytes 4194304 | tf_op jit(solution)/shard_map/all_to_all | solution.py:43
  45.8 0.8 copy.28
  46.6 0.8 copy.29
  47.6 1.1 copy.23
  48.8 3.0 %copy.26 = bf16[2,128,8,512]{1,0,2,3:T(2,128)(2,1)S(1)} copy(bf16[2,128,8,512]{1,0,3,2:T(2,128)(2,1)} %bitcast.62) | data formatting | bytes 4194304 | tf_op jit(solution)/shard_map/all_to_all | solution.py:51
  51.8 0.9 convolution_bitcast_fusion.2
  52.7 19.2 %all-to-all-done = bf16[2,128,4096]{1,0,2:T(2,128)(2,1)S(1)} async-done(((bf16[2,128,4096]{1,0,2:T(2,128)(2,1)}), bf16[2,128,4096]{1,0,2:T(2,128)(2,1)S(1)}, u32[]{:S(2)}, u32[]{:S(2)}) %all-to-all-start) | async-done | bytes 2097184 | tf_op jit(solution)/shard_map/all_to_all | solution.py:43
  72.0 1.4 copy.21
  73.4 0.9 convolution_bitcast_fusion.3
  74.3 78.4 %all-reduce = (f32[16,16]{1,0:T(8,128)S(1)}, f32[16,16]{1,0:T(8,128)S(1)}) all-reduce(f32[16,16]{1,0:T(8,128)S(1)} %convolution_bitcast_fusion.3, f32[16,16]{1,0:T(8,128)S(1)} %convolution_bitcast_fusion.2), channel_id=1, replica_groups=mesh['task'=8,'fsdp'=32] {'task','fsdp'}, use_global_device_ids=true, to_apply=%region_0.0 | all-reduce | flops 512 | bytes 4096 | tf_op jit(solution)/shard_map/psum | solution.py:78
  155.2 1.3 broadcast_divide_fusion
  156.5 29.4 %while.29 = (s32[]{:T(128)}, f32[16]{0:T(128)S(1)}, f32[16,16]{1,0:T(8,128)S(1)}, s32[]{:T(128)}, s32[]{:T(128)}, /*index=5*/f32[]{:T(128)}) while((s32[]{:T(128)}, f32[16]{0:T(128)S(1)}, f32[16,16]{1,0:T(8,128)S(1)}, s32[]{:T(128)}, s32[]{:T(128)}, /*index=5*/f32[]{:T(128)}) %tuple.78), condition=%wide.region_10.11_spmd.clone, body=%wide.region_8.10_spmd.clone.sunk | while | flops 3237 | bytes 1468 | solution.py:26
  156.6 0.7 fusion.31
  158.0 0.7 fusion.31
  159.5 0.7 fusion.31
  161.0 0.7 fusion.31
  162.4 0.7 fusion.31
  163.9 0.7 fusion.31
  165.4 0.7 fusion.31
  166.9 0.7 fusion.31
  168.3 0.7 fusion.31
  169.8 0.7 fusion.31
  171.3 0.7 fusion.31
  174.2 0.7 fusion.31
  175.7 0.7 fusion.31
  177.2 0.7 fusion.31
  178.6 0.7 fusion.31
  180.1 0.7 fusion.31
  181.6 0.7 fusion.31
  183.1 0.7 fusion.31
  184.5 0.7 fusion.31
  186.1 4.7 %multiply_reduce_fusion = f32[128,512]{0,1:T(8,128)S(1)} fusion(f32[8,2]{1,0:T(8,128)S(1)} %mul.109, bf16[2,128,8,512]{1,0,3,2:T(2,128)(2,1)} %bitcast.63), kind=kLoop, calls=%fused_computation.22 | loop fusion | flops 3080192 | bytes 2359360 | tf_op jit(solution)/shard_map/reduce_sum | solution.py:39
  190.7 0.8 copy.34
  191.6 2.0 divide_subtract_fusion.2
  193.6 1.8 copy.35
  195.4 1.8 copy.36
  197.1 1.8 copy.37
  198.9 29.4 %while.28 = (s32[]{:T(128)}, f32[16]{0:T(128)S(1)}, f32[16,16]{1,0:T(8,128)S(1)}, s32[]{:T(128)}, s32[]{:T(128)}, /*index=5*/f32[]{:T(128)}) while((s32[]{:T(128)}, f32[16]{0:T(128)S(1)}, f32[16,16]{1,0:T(8,128)S(1)}, s32[]{:T(128)}, s32[]{:T(128)}, /*index=5*/f32[]{:T(128)}) %tuple.75), condition=%wide.region_4.0_spmd.clone, body=%wide.region_2.0_spmd.clone.sunk | while | flops 3237 | bytes 1468 | solution.py:26
  200.4 0.7 fusion.29
  201.9 0.7 fusion.29
  203.3 0.7 fusion.29
  206.3 0.7 fusion.29
  207.8 0.7 fusion.29
  209.2 0.7 fusion.29
  212.2 0.7 fusion.29
  213.6 0.7 fusion.29
  215.1 0.7 fusion.29
  218.1 0.7 fusion.29
  219.5 0.7 fusion.29
  221.0 0.7 fusion.29
  222.5 0.7 fusion.29
  223.9 0.7 fusion.29
  225.4 0.7 fusion.29
  226.9 0.7 fusion.29
  228.4 3.1 %multiply_reduce_fusion.1 = f32[128,512]{0,1:T(8,128)S(1)} fusion(f32[8,2]{1,0:T(8,128)S(1)} %mul.100, bf16[2,128,8,512]{1,0,3,2:T(2,128)(2,1)S(1)} %bitcast.61), kind=kLoop, calls=%fused_computation.23 | loop fusion | flops 3080192 | bytes 2359360 | tf_op jit(solution)/shard_map/reduce_sum | solution.py:39
  231.5 0.8 copy.30
  232.5 0.8 copy.31
  233.4 0.8 copy.32
  234.2 0.8 copy.33
  (69 shorter events, 33.5 us)
Async XLA Ops:
  6.8 33.1 %all-to-all-start.1 = ((bf16[2,128,4096]{1,0,2:T(2,128)(2,1)}), bf16[2,128,4096]{1,0,2:T(2,128)(2,1)S(1)}, u32[]{:S(2)}, u32[]{:S(2)}) async-start(bf16[2,128,4096]{1,0,2:T(2,128)(2,1)} %copy.25), calls=%async_computation.1 | async-start | bytes 4194304 | tf_op jit(solution)/shard_map/all_to_all | solution.py:51
  19.7 25.9 %copy-start.1 = (f32[128,512]{1,0:T(8,128)S(1)}, f32[128,512]{1,0:T(8,128)}, u32[]{:S(2)}) copy-start(f32[128,512]{1,0:T(8,128)} %param.18) | copy-start | bytes 786436
  19.7 26.0 %copy-start.2 = (f32[128,512]{1,0:T(8,128)S(1)}, f32[128,512]{1,0:T(8,128)}, u32[]{:S(2)}) copy-start(f32[128,512]{1,0:T(8,128)} %param.19) | copy-start | bytes 786436
  19.7 26.9 %copy-start.3 = (f32[128,512]{1,0:T(8,128)S(1)}, f32[128,512]{1,0:T(8,128)}, u32[]{:S(2)}) copy-start(f32[128,512]{1,0:T(8,128)} %param.17) | copy-start | bytes 786436
  19.7 27.7 %copy-start.4 = (f32[128,512]{1,0:T(8,128)S(1)}, f32[128,512]{1,0:T(8,128)}, u32[]{:S(2)}) copy-start(f32[128,512]{1,0:T(8,128)} %param.14) | copy-start | bytes 786436
  39.9 1.3 copy-start
  41.2 30.7 %all-to-all-start = ((bf16[2,128,4096]{1,0,2:T(2,128)(2,1)}), bf16[2,128,4096]{1,0,2:T(2,128)(2,1)S(1)}, u32[]{:S(2)}, u32[]{:S(2)}) async-start(bf16[2,128,4096]{1,0,2:T(2,128)(2,1)} %copy.20), calls=%async_computation | async-start | bytes 4194304 | tf_op jit(solution)/shard_map/all_to_all | solution.py:43
  45.7 2.9 %copy-start.5 = (f32[128,512]{1,0:T(8,128)S(1)}, f32[128,512]{1,0:T(8,128)}, u32[]{:S(2)}) copy-start(f32[128,512]{1,0:T(8,128)} %param.13) | copy-start | bytes 786436
where the time goes:
time: 236 us; the launch traced here: 235 us
  blocking collectives  78.4 us (33%)
  waiting for transfers between devices  39.4 us (17%)
  other arithmetic  38.9 us (16%)
  local copies, waits for them, and re-layouts  32.3 us (14%)
  matrix products  31.6 us (13%)
  starting transfers between devices  11.1 us (5%)
  loops' own time  2.61 us (1%)
    psum x1, blocking collectives, local(): lax.psum((partial_first, partial_second), ('task', 'fsdp'))  78.4 us
    dot_general x40, matrix products, advance(): slope = 2.0 * jnp.dot(scaled, mixture, precision=lax.Precision.HIGHEST)  29.8 us
    add x40, other arithmetic, advance(): return mixture + stepsize * (vertex - mixture)  26.5 us
    unnamed x28, local copies, waits for them, and re-layouts  26.3 us
    all_to_all x1, waiting for transfers between devices, prepare_second(): lax.all_to_all(gradients, 'task', split_axis=2, concat_axis=0, tiled=True)  20.2 us
    all_to_all x1, waiting for transfers between devices, prepare_first(): lax.all_to_all(gradients, 'task', split_axis=2, concat_axis=0, tiled=True)  19.2 us
    reduce_sum x2, other arithmetic, weighted_sum(): return jnp.sum(mixture[:, None, None] * stacked.astype(jnp.float32), axis=0)  7.72 us
    all_to_all x1, starting transfers between devices, prepare_second(): lax.all_to_all(gradients, 'task', split_axis=2, concat_axis=0, tiled=True)  6.74 us
  transfers between devices with their start and end apart: 2, of which 2 were waited for; matrix products, arithmetic and copies ran while one was open for 6% of the time, Pallas kernels for 0%

commit v1 on v0

--- a/solution.py
+++ b/solution.py
@@ -2,6 +2,7 @@
 import jax.numpy as jnp
 from jax import lax
 from jax.sharding import PartitionSpec as P
+from jax.lax import psum
 
 ITERS = 20
 temper = 0.05
@@ -75,7 +76,9 @@
 ):
     retained_first, partial_first = prepare_first(grads_first)
     retained_second, partial_second = prepare_second(grads_second)
-    gram_first, gram_second = lax.psum((partial_first, partial_second), ("task", "fsdp"))
+    gram_first, gram_second = psum(
+        psum((partial_first, partial_second), axis_name="task"), axis_name="fsdp"
+    )
     mixture_first = frank_wolfe(gram_first)
     mixture_second = frank_wolfe(gram_second)
     combined_first = combine_first(retained_first, mixture_first)

time: 236 us -> 324 us (1.37)
  the two profiles are of different devices: /device:TPU:1 before, /device:TPU:0 now
where the time goes in v1:
time: 324 us; the launch traced here: 323 us
  blocking collectives  169 us (52%)
  waiting for transfers between devices  40.9 us (13%)
  other arithmetic  38.9 us (12%)
  local copies, waits for them, and re-layouts  32.3 us (10%)
  matrix products  31.6 us (10%)
  starting transfers between devices  7.2 us (2%)
    psum x1, blocking collectives, local(): psum(psum((partial_first, partial_second), axis_name='task'), axis_name='...  145 us
    dot_general x40, matrix products, advance(): slope = 2.0 * jnp.dot(scaled, mixture, precision=lax.Precision.HIGHEST)  29.8 us
    add x40, other arithmetic, advance(): return mixture + stepsize * (vertex - mixture)  26.5 us
    unnamed x28, local copies, waits for them, and re-layouts  26.3 us
    psum x1, blocking collectives, local(): psum((partial_first, partial_second), axis_name='task')  23.8 us
    all_to_all x1, waiting for transfers between devices, prepare_second(): lax.all_to_all(gradients, 'task', split_axis=2, concat_axis=0, tiled=True)  20.9 us
    all_to_all x1, waiting for transfers between devices, prepare_first(): lax.all_to_all(gradients, 'task', split_axis=2, concat_axis=0, tiled=True)  20 us
    reduce_sum x2, other arithmetic, weighted_sum(): return jnp.sum(mixture[:, None, None] * stacked.astype(jnp.float32), axis=0)  7.72 us
  transfers between devices with their start and end apart: 2, of which 2 were waited for; matrix products, arithmetic and copies ran while one was open for 4% of the time, Pallas kernels for 0%

profile of v1, /device:TPU:0, one launch (start us, length us, event | category | flops | bytes accessed | tf_op | source)
XLA Modules:
  0.0 323.3 jit_solution(11171397481924810321)
XLA Ops:
  0.6 6.2 %copy.25 = bf16[2,128,4096]{1,0,2:T(2,128)(2,1)} copy(bf16[2,128,4096]{2,1,0:T(8,128)(2,1)} %param.16) | data formatting | bytes 4194304 | tf_op args[4]
  6.8 3.6 %all-to-all-start.1 = ((bf16[2,128,4096]{1,0,2:T(2,128)(2,1)}), bf16[2,128,4096]{1,0,2:T(2,128)(2,1)S(1)}, u32[]{:S(2)}, u32[]{:S(2)}) async-start(bf16[2,128,4096]{1,0,2:T(2,128)(2,1)} %copy.25), calls=%async_computation.1 | async-start | bytes 4194304 | tf_op jit(solution)/shard_map/all_to_all | solution.py:52
  10.4 6.2 %copy.20 = bf16[2,128,4096]{1,0,2:T(2,128)(2,1)} copy(bf16[2,128,4096]{2,1,0:T(8,128)(2,1)} %param.12) | data formatting | bytes 4194304 | tf_op args[0]
  16.6 20.9 %all-to-all-done.1 = bf16[2,128,4096]{1,0,2:T(2,128)(2,1)S(1)} async-done(((bf16[2,128,4096]{1,0,2:T(2,128)(2,1)}), bf16[2,128,4096]{1,0,2:T(2,128)(2,1)S(1)}, u32[]{:S(2)}, u32[]{:S(2)}) %all-to-all-start.1) | async-done | bytes 2097184 | tf_op jit(solution)/shard_map/all_to_all | solution.py:52
  37.6 1.3 copy-done
  38.9 3.6 %all-to-all-start = ((bf16[2,128,4096]{1,0,2:T(2,128)(2,1)}), bf16[2,128,4096]{1,0,2:T(2,128)(2,1)S(1)}, u32[]{:S(2)}, u32[]{:S(2)}) async-start(bf16[2,128,4096]{1,0,2:T(2,128)(2,1)} %copy.20), calls=%async_computation | async-start | bytes 4194304 | tf_op jit(solution)/shard_map/all_to_all | solution.py:44
  42.6 0.8 copy.28
  43.5 0.8 copy.29
  44.5 1.1 copy.23
  45.7 3.0 copy.26
  48.7 0.9 convolution_bitcast_fusion.2
  49.6 20.0 %all-to-all-done = bf16[2,128,4096]{1,0,2:T(2,128)(2,1)S(1)} async-done(((bf16[2,128,4096]{1,0,2:T(2,128)(2,1)}), bf16[2,128,4096]{1,0,2:T(2,128)(2,1)S(1)}, u32[]{:S(2)}, u32[]{:S(2)}) %all-to-all-start) | async-done | bytes 2097184 | tf_op jit(solution)/shard_map/all_to_all | solution.py:44
  69.6 1.4 copy.21
  71.0 0.9 convolution_bitcast_fusion.3
  71.9 23.8 %all-reduce.1 = (f32[16,16]{1,0:T(8,128)S(1)}, f32[16,16]{1,0:T(8,128)S(1)}) all-reduce(f32[16,16]{1,0:T(8,128)S(1)} %convolution_bitcast_fusion.3, f32[16,16]{1,0:T(8,128)S(1)} %convolution_bitcast_fusion.2), channel_id=1, replica_groups=mesh['task'=8,'fsdp'=32] {'task'}, use_global_device_ids=true, to_apply=%region_0.0 | all-reduce | flops 512 | bytes 4096 | tf_op jit(solution)/shard_map/psum | solution.py:80
  95.8 145.2 %all-reduce = (f32[16,16]{1,0:T(8,128)S(1)}, f32[16,16]{1,0:T(8,128)S(1)}) all-reduce(f32[16,16]{1,0:T(8,128)S(1)} %get-tuple-element.184, f32[16,16]{1,0:T(8,128)S(1)} %get-tuple-element.185), channel_id=1, replica_groups=mesh['task'=8,'fsdp'=32] {'fsdp'}, use_global_device_ids=true, to_apply=%region_1.0 | all-reduce | flops 512 | bytes 4096 | tf_op jit(solution)/shard_map/psum | solution.py:79
  243.5 1.3 broadcast_divide_fusion
  244.8 29.4 %while.29 = (s32[]{:T(128)}, f32[16]{0:T(128)S(1)}, f32[16,16]{1,0:T(8,128)S(1)}, s32[]{:T(128)}, s32[]{:T(128)}, /*index=5*/f32[]{:T(128)}) while((s32[]{:T(128)}, f32[16]{0:T(128)S(1)}, f32[16,16]{1,0:T(8,128)S(1)}, s32[]{:T(128)}, s32[]{:T(128)}, /*index=5*/f32[]{:T(128)}) %tuple.78), condition=%wide.region_12.13_spmd.clone, body=%wide.region_10.12_spmd.clone.sunk | while | flops 3237 | bytes 1468 | solution.py:27
  244.8 0.7 fusion.31
  246.3 0.7 fusion.31
  247.8 0.7 fusion.31
  249.2 0.7 fusion.31
  250.7 0.7 fusion.31
  252.2 0.7 fusion.31
  253.7 0.7 fusion.31
  255.1 0.7 fusion.31
  256.6 0.7 fusion.31
  258.1 0.7 fusion.31
  259.5 0.7 fusion.31
  261.0 0.7 fusion.31
  262.5 0.7 fusion.31
  264.0 0.7 fusion.31
  265.4 0.7 fusion.31
  268.4 0.7 fusion.31
  269.8 0.7 fusion.31
  271.3 0.7 fusion.31
  274.3 4.7 %multiply_reduce_fusion = f32[128,512]{0,1:T(8,128)S(1)} fusion(f32[8,2]{1,0:T(8,128)S(1)} %mul.109, bf16[2,128,8,512]{1,0,3,2:T(2,128)(2,1)} %bitcast.63), kind=kLoop, calls=%fused_computation.22 | loop fusion | flops 3080192 | bytes 2359360 | tf_op jit(solution)/shard_map/reduce_sum | solution.py:40
  279.0 0.8 copy.34
  279.8 2.0 divide_subtract_fusion.2
  281.8 1.8 copy.35
  283.6 1.8 copy.36
  285.4 1.8 copy.37
  287.2 29.4 %while.28 = (s32[]{:T(128)}, f32[16]{0:T(128)S(1)}, f32[16,16]{1,0:T(8,128)S(1)}, s32[]{:T(128)}, s32[]{:T(128)}, /*index=5*/f32[]{:T(128)}) while((s32[]{:T(128)}, f32[16]{0:T(128)S(1)}, f32[16,16]{1,0:T(8,128)S(1)}, s32[]{:T(128)}, s32[]{:T(128)}, /*index=5*/f32[]{:T(128)}) %tuple.75), condition=%wide.region_5.6_spmd.clone, body=%wide.region_3.5_spmd.clone.sunk | while | flops 3237 | bytes 1468 | solution.py:27
  290.1 0.7 fusion.29
  291.6 0.7 fusion.29
  293.1 0.7 fusion.29
  294.6 0.7 fusion.29
  296.0 0.7 fusion.29
  297.5 0.7 fusion.29
  299.0 0.7 fusion.29
  300.4 0.7 fusion.29
  301.9 0.7 fusion.29
  303.4 0.7 fusion.29
  306.3 0.7 fusion.29
  307.8 0.7 fusion.29
  309.3 0.7 fusion.29
  312.2 0.7 fusion.29
  313.7 0.7 fusion.29
  315.2 0.7 fusion.29
  316.7 3.1 multiply_reduce_fusion.1
  319.8 0.8 copy.30
  320.8 0.8 copy.31
  321.6 0.8 copy.32
  322.5 0.8 copy.33
  (70 shorter events, 34.2 us)
Async XLA Ops:
  6.8 30.7 %all-to-all-start.1 = ((bf16[2,128,4096]{1,0,2:T(2,128)(2,1)}), bf16[2,128,4096]{1,0,2:T(2,128)(2,1)S(1)}, u32[]{:S(2)}, u32[]{:S(2)}) async-start(bf16[2,128,4096]{1,0,2:T(2,128)(2,1)} %copy.25), calls=%async_computation.1 | async-start | bytes 4194304 | tf_op jit(solution)/shard_map/all_to_all | solution.py:52
  16.6 25.9 %copy-start.1 = (f32[128,512]{1,0:T(8,128)S(1)}, f32[128,512]{1,0:T(8,128)}, u32[]{:S(2)}) copy-start(f32[128,512]{1,0:T(8,128)} %param.18) | copy-start | bytes 786436
  16.6 26.0 %copy-start.2 = (f32[128,512]{1,0:T(8,128)S(1)}, f32[128,512]{1,0:T(8,128)}, u32[]{:S(2)}) copy-start(f32[128,512]{1,0:T(8,128)} %param.19) | copy-start | bytes 786436
  16.6 26.9 %copy-start.3 = (f32[128,512]{1,0:T(8,128)S(1)}, f32[128,512]{1,0:T(8,128)}, u32[]{:S(2)}) copy-start(f32[128,512]{1,0:T(8,128)} %param.17) | copy-start | bytes 786436
  16.6 27.7 %copy-start.4 = (f32[128,512]{1,0:T(8,128)S(1)}, f32[128,512]{1,0:T(8,128)}, u32[]{:S(2)}) copy-start(f32[128,512]{1,0:T(8,128)} %param.14) | copy-start | bytes 786436
  37.6 1.3 copy-start
  38.9 30.7 %all-to-all-start = ((bf16[2,128,4096]{1,0,2:T(2,128)(2,1)}), bf16[2,128,4096]{1,0,2:T(2,128)(2,1)S(1)}, u32[]{:S(2)}, u32[]{:S(2)}) async-start(bf16[2,128,4096]{1,0,2:T(2,128)(2,1)} %copy.20), calls=%async_computation | async-start | bytes 4194304 | tf_op jit(solution)/shard_map/all_to_all | solution.py:44
  42.6 2.9 copy-start.5
